TPU v7x, 256 devices: a whole 4x4x8 slice. The times are simulated.
256 devices in a mesh: dp: 8 (over y, core), expert: 32 (over x, z).
Axes of the slice: x: 4, y: 4, z: 8, core: 2. Of those that a mesh axis runs over, the one named last changes fastest.
Arguments:
- tokens: bfloat16 [2048, 3584], P(('dp', 'expert')), may hold values from -6 to 6
- routes: int32 [2048, 8], P(('dp', 'expert')), may hold values from 0 to 63, all different within a row; in each aligned block of 8 rows (0 to 7, 8 to 15, ...) at most 2 rows name the same one
- gates: bfloat16 [2048, 8], P(('dp', 'expert')), may hold values from 0.049804688 to 0.5
- cotangent: bfloat16 [2048, 3584], P(('dp', 'expert')), may hold values from -1.5 to 1.5
- w_gate: bfloat16 [64, 3584, 1024], P('expert', None, 'dp'), may hold values from -0.09375 to 0.09375
- w_up: bfloat16 [64, 3584, 1024], P('expert', None, 'dp'), may hold values from -0.09375 to 0.09375
- w_down: bfloat16 [64, 1024, 3584], P('expert', 'dp'), may hold values from -0.1875 to 0.1875
Outputs:
- token_grads: bfloat16 [2048, 3584], P(('dp', 'expert'))
- gate_grads: float32 [2048, 8], P(('dp', 'expert'))
- grad_gate: bfloat16 [64, 3584, 1024], P('expert', None, 'dp')
- grad_up: bfloat16 [64, 3584, 1024], P('expert', None, 'dp')
- grad_down: bfloat16 [64, 1024, 3584], P('expert', 'dp')
Inputs may be any that keep to these rules, and one draw needn't show every extreme that they name: `routes`: each row names 8 different experts. Within each device's block of 8 rows no expert is named by more than 2 rows, a bound that some block reaches.
All inputs are finite; a program needn't handle non-finite values.
Results may differ from a plain program's by a relative error of at most 0.0058.
Values may be sent and summed in bfloat16 or wider, within the bound.
A program may use at most 192 MiB of HBM per device.

v0:
```python
from functools import partial
import jax
import jax.numpy as jnp
from jax import lax
from jax.sharding import PartitionSpec as P

TOPK = 8


def route_table(routes, experts_all, capacity):
    pairs = routes.reshape(-1)
    onehot = (pairs[:, None] == jnp.arange(experts_all, dtype=jnp.int32)[None, :]).astype(jnp.int32)
    before = jnp.cumsum(onehot, axis=0) - onehot
    within = jnp.sum(before * onehot, axis=1)
    target = pairs * capacity + within
    slot_ids = jnp.arange(experts_all * capacity, dtype=jnp.int32)
    return (target[:, None] == slot_ids[None, :]).astype(jnp.float32)


def dispatch(table, tokens, cotangent, gates):
    count = tokens.shape[0]
    slots = table.shape[1]
    spread = table.reshape(count, TOPK, slots).sum(axis=1).astype(jnp.bfloat16)
    both = jnp.concatenate([tokens, cotangent], axis=1)
    slot_rows = jnp.einsum("ts,td->sd", spread, both, preferred_element_type=jnp.float32).astype(
        jnp.bfloat16
    )
    flat_gates = gates.reshape(-1).astype(jnp.float32)
    slot_gates = jnp.einsum("ps,p->s", table, flat_gates, precision=lax.Precision.HIGHEST).astype(
        jnp.bfloat16
    )
    pad = jnp.zeros((slots, 127), jnp.bfloat16)
    return jnp.concatenate([slot_rows, slot_gates[:, None], pad], axis=1)


def expert_one(rows_in, cot_in, row_gate, w_gate, w_up, w_down):
    gate_pre = jnp.dot(rows_in, w_gate, preferred_element_type=jnp.float32)
    upper_pre = jnp.dot(rows_in, w_up, preferred_element_type=jnp.float32)
    gate_sig = jax.nn.sigmoid(gate_pre)
    active = (gate_pre * gate_sig * upper_pre).astype(jnp.bfloat16)
    output = jnp.dot(active, w_down, preferred_element_type=jnp.float32)
    cot_float = cot_in.astype(jnp.float32)
    gate_part = jnp.sum(output * cot_float, axis=-1)
    scaled = (row_gate.astype(jnp.float32)[:, None] * cot_float).astype(jnp.bfloat16)
    grad_active = lax.dot_general(
        scaled, w_down, (((1,), (1,)), ((), ())), preferred_element_type=jnp.float32
    )
    grad_upper = (grad_active * gate_pre * gate_sig).astype(jnp.bfloat16)
    grad_gpre = (grad_active * upper_pre * gate_sig * (1.0 + gate_pre * (1.0 - gate_sig))).astype(
        jnp.bfloat16
    )
    token_part = lax.dot_general(
        grad_gpre, w_gate, (((1,), (1,)), ((), ())), preferred_element_type=jnp.float32
    )
    token_part = token_part + lax.dot_general(
        grad_upper, w_up, (((1,), (1,)), ((), ())), preferred_element_type=jnp.float32
    )
    grad_g = lax.dot_general(
        rows_in, grad_gpre, (((0,), (0,)), ((), ())), preferred_element_type=jnp.float32
    ).astype(jnp.bfloat16)
    grad_u = lax.dot_general(
        rows_in, grad_upper, (((0,), (0,)), ((), ())), preferred_element_type=jnp.float32
    ).astype(jnp.bfloat16)
    grad_d = lax.dot_general(
        active, scaled, (((0,), (0,)), ((), ())), preferred_element_type=jnp.float32
    ).astype(jnp.bfloat16)
    return (token_part, gate_part, grad_g, grad_u, grad_d)


def local(tokens, routes, gates, cotangent, w_gate, w_up, w_down):
    n_expert = lax.axis_size("expert")
    n_groups = lax.axis_size("dp")
    local_experts = w_gate.shape[0]
    experts_all = local_experts * n_expert
    tok_count = tokens.shape[0]
    width = tokens.shape[1]
    capacity = 16 * tok_count // experts_all
    slots = experts_all * capacity
    per_dest = local_experts * capacity
    table = route_table(routes, experts_all, capacity)
    send = dispatch(table, tokens, cotangent, gates)
    send = send.reshape(n_expert, per_dest, send.shape[-1])
    recv = lax.all_to_all(send, "expert", split_axis=0, concat_axis=0, tiled=True)
    recv = lax.all_gather(recv, "dp", axis=0, tiled=True)
    rows = n_groups * n_expert
    parts, gparts, grads_g, grads_u, grads_d = ([], [], [], [], [])
    for j in range(local_experts):
        block = recv[:, j * capacity : (j + 1) * capacity, :].reshape(rows * capacity, -1)
        token_part, gate_part, grad_g, grad_u, grad_d = expert_one(
            block[:, :width],
            block[:, width : 2 * width],
            block[:, 2 * width],
            w_gate[j],
            w_up[j],
            w_down[j],
        )
        token_part = token_part.reshape(n_groups, n_expert * capacity, width)
        part = lax.psum_scatter(token_part, "dp", scatter_dimension=0, tiled=False)
        parts.append(part.reshape(n_expert, capacity, width))
        gparts.append(gate_part.reshape(n_groups, n_expert, capacity))
        grads_g.append(grad_g)
        grads_u.append(grad_u)
        grads_d.append(grad_d)
    token_part = jnp.stack(parts, axis=1).reshape(n_expert, local_experts, capacity, width)
    gate_part = jnp.stack(gparts, axis=2).reshape(n_groups, n_expert * per_dest)
    gate_part = lax.psum_scatter(gate_part, "dp", scatter_dimension=0, tiled=False)
    gate_part = gate_part.reshape(n_expert, per_dest)
    back_tokens, back_gates = (
        lax.all_to_all(token_part, "expert", split_axis=0, concat_axis=0, tiled=True),
        lax.all_to_all(gate_part, "expert", split_axis=0, concat_axis=0, tiled=True),
    )
    back_tokens = back_tokens.reshape(slots, width)
    back_gates = back_gates.reshape(slots)
    spread = table.reshape(tok_count, TOPK, slots).sum(axis=1)
    token_sum = jnp.einsum("ts,sd->td", spread, back_tokens, precision=lax.Precision.HIGHEST)
    gate_sum = jnp.einsum("ps,s->p", table, back_gates, precision=lax.Precision.HIGHEST)
    token_grads = token_sum.astype(jnp.bfloat16)
    gate_grads = gate_sum.reshape(tok_count, TOPK)
    grad_gate = jnp.stack(grads_g, axis=0)
    grad_up = jnp.stack(grads_u, axis=0)
    grad_down = jnp.stack(grads_d, axis=0)
    return (token_grads, gate_grads, grad_gate, grad_up, grad_down)


def solution(mesh):
    return jax.shard_map(
        local,
        mesh=mesh,
        in_specs=(
            P(("dp", "expert"), None),
            P(("dp", "expert"), None),
            P(("dp", "expert"), None),
            P(("dp", "expert"), None),
            P("expert", None, "dp"),
            P("expert", None, "dp"),
            P("expert", "dp", None),
        ),
        out_specs=(
            P(("dp", "expert"), None),
            P(("dp", "expert"), None),
            P("expert", None, "dp"),
            P("expert", None, "dp"),
            P("expert", "dp", None),
        ),
        check_vma=False,
    )
```

profile of v0, /device:TPU:32, one launch (start us, length us, event | category | flops | bytes accessed | tf_op | source)
XLA Modules:
  0.0 374.6 jit_solution(2525341771582631884)
XLA Ops:
  7.2 0.8 eq.57
  8.1 0.1 reduce_window_sum.11
  8.2 0.2 select_reduce_fusion
  8.4 0.7 multiply_add_fusion
  9.1 0.6 copy-done.8
  9.8 0.6 copy-done.6
  10.4 1.5 convolution_convert_fusion
  11.9 1.6 concatenate.12
  13.6 0.2 fusion.22
  13.8 0.2 concatenate.15
  14.1 5.0 %concatenate.14 = bf16[32,4,7296]{2,1,0:T(4,128)(2,1)S(1)} concatenate(bf16[32,4,7168]{2,1,0:T(4,128)(2,1)} %concatenate.12, bf16[32,4,1]{2,1,0:T(4,128)(2,1)S(1)} %concatenate.15, bf16[32,4,127]{2,1,0:T(4,128)(2,1)S(1)} %broadcast_in_dim.2), dimensions={2} | concatenate | bytes 3735552 | tf_op jit(solution)/shard_map/concatenate | solution.py:33
  19.1 57.3 %all_to_all.19 = bf16[32,4,7296]{2,1,0:T(4,128)(2,1)} all-to-all(bf16[32,4,7296]{2,1,0:T(4,128)(2,1)S(1)} %concatenate.14), channel_id=1, replica_groups=mesh['dp'=8,'expert'=32] {'expert'}, dimensions={0} | all-to-all | bytes 3735552 | tf_op jit(solution)/shard_map/all_to_all | solution.py:83
  76.5 76.3 %all-gather.2.cloned.1.call-done = bf16[256,4,7296]{2,1,0:T(4,128)(2,1)} async-done(((bf16[32,4,7296]{2,1,0:T(4,128)(2,1)}), bf16[256,4,7296]{2,1,0:T(4,128)(2,1)}) %all-gather.2.cloned.1.call-update) | async-done | bytes 14942224 | tf_op jit(solution)/shard_map/all_gather | solution.py:84
  152.8 16.6 %fusion.66 = (bf16[256,2,7296]{2,1,0:T(2,128)(2,1)}, bf16[256,2,7296]{2,1,0:T(2,128)(2,1)}) fusion(bf16[256,4,7296]{2,1,0:T(4,128)(2,1)} %all-gather.2.cloned.1.call-done), kind=kLoop, calls=%fused_computation.100 | loop fusion | bytes 29884416 | tf_op jit(solution)/shard_map/slice | solution.py:88
  169.4 15.7 %reshape.89 = bf16[512,7296]{1,0:T(8,128)(2,1)} reshape(bf16[256,2,7296]{2,1,0:T(2,128)(2,1)} %get-tuple-element.5) | data formatting | bytes 14942208 | tf_op jit(solution)/shard_map/reshape | solution.py:88
  185.1 1.2 convert_reduce_fusion.1
  186.3 3.3 fusion.18
  189.7 3.4 fusion.27
  193.0 0.1 copy-done.1
  193.2 1.1 multiply_convert_fusion.1
  194.3 1.1 fusion.36
  195.5 4.1 %convolution_add_fusion.1 = f32[512,3584]{1,0:T(8,128)} fusion(f32[512,3584]{1,0:T(8,128)S(1)} %fusion.36, bf16[512,128]{1,0:T(8,128)(2,1)S(1)} %get-tuple-element.9, bf16[2,3584,128]{2,1,0:T(8,128)(2,1)S(1)} %copy-done.1), kind=kOutput, calls=%fused_computation.10 | convolution fusion | flops 471597056 | bytes 15728640 | tf_op jit(solution)/shard_map/dot_general | solution.py:55
  199.6 0.2 reduce-scatter.6.cloned.1.call-start
  199.8 15.7 %reshape.91 = bf16[512,7296]{1,0:T(8,128)(2,1)} reshape(bf16[256,2,7296]{2,1,0:T(2,128)(2,1)} %get-tuple-element.6) | data formatting | bytes 14942208 | tf_op jit(solution)/shard_map/reshape | solution.py:88
  215.5 1.2 convert_reduce_fusion
  216.7 3.4 fusion.12
  220.1 3.4 fusion.24
  223.5 0.3 copy-done.2
  223.8 1.1 multiply_convert_fusion
  225.0 1.1 fusion.29
  226.1 4.1 %convolution_add_fusion = f32[512,3584]{1,0:T(8,128)} fusion(f32[512,3584]{1,0:T(8,128)S(1)} %fusion.29, bf16[512,128]{1,0:T(8,128)(2,1)S(1)} %get-tuple-element.12, bf16[2,3584,128]{2,1,0:T(8,128)(2,1)S(1)} %copy-done.2), kind=kOutput, calls=%fused_computation.9 | convolution fusion | flops 471597056 | bytes 15728640 | tf_op jit(solution)/shard_map/dot_general | solution.py:55
  230.2 0.6 copy-done.18
  230.9 0.6 dynamic-slice
  231.5 0.3 copy-done.17
  231.8 3.3 fusion.1
  235.0 0.1 stack_reshape.6
  235.2 3.3 fusion.3
  238.5 0.1 stack_reshape.7
  238.7 0.5 copy.21
  239.2 25.2 %all-reduce = f32[8,128]{0,1:T(8,128)S(1)} all-reduce(f32[8,128]{0,1:T(8,128)S(1)} %bitcast.88), channel_id=4, replica_groups=mesh['dp'=8,'expert'=32] {'dp'}, use_global_device_ids=true, to_apply=%region_7.8.clone | all-reduce | flops 1024 | bytes 8192
  264.4 0.8 dynamic-slice_reduce_fusion
  265.2 0.7 all_to_all.14
  266.0 10.1 %all-to-all-start.2 = ((f32[32,1,4]{2,1,0:T(1,128)}), f32[32,1,4]{2,1,0:T(1,128)S(1)}, u32[]{:S(2)}, u32[]{:S(2)}) async-start(f32[32,1,4]{2,1,0:T(1,128)} %bitcast.11), calls=%async_computation.4 | async-start | bytes 32768 | tf_op jit(solution)/shard_map/all_to_all | solution.py:110
  276.1 2.7 stack_reshape_reduce_scatter.6
  278.7 24.2 %reduce-scatter.6.cloned.1.call-done = f32[1,64,3584]{2,1,0:T(8,128)} async-done(((f32[8,64,3584]{2,1,0:T(8,128)}), f32[1,64,3584]{2,1,0:T(8,128)}) %reduce-scatter.6.cloned.1.call-update) | async-done | bytes 917520 | tf_op jit(solution)/shard_map/reduce_scatter | solution.py:98
  302.9 2.6 stack_reshape_reduce_scatter.7
  305.6 3.8 %pad_maximum_fusion = f32[32,2,2,3584]{3,2,1,0:T(2,128)} fusion(f32[32,1,2,3584]{3,2,1,0:T(2,128)} %stack_reshape_reduce_scatter.7, f32[32,1,2,3584]{3,2,1,0:T(2,128)} %stack_reshape_reduce_scatter.6), kind=kLoop, calls=%fused_computation.36 | loop fusion | flops 458752 | bytes 3670016 | tf_op jit(solution)/shard_map/stack | solution.py:104
  309.3 10.3 %all-to-all-start.1 = ((f32[32,2,2,3584]{3,2,1,0:T(2,128)}), f32[32,2,2,3584]{3,2,1,0:T(2,128)}, u32[]{:S(2)}, u32[]{:S(2)}) async-start(f32[32,2,2,3584]{3,2,1,0:T(2,128)} %pad_maximum_fusion), calls=%async_computation.3 | async-start | bytes 3670016 | tf_op jit(solution)/shard_map/all_to_all | solution.py:109
  319.7 3.4 fusion.6
  323.1 1.2 fusion.4
  324.3 1.2 slice-done.7
  325.5 1.2 fusion.5
  326.7 1.2 fusion.7
  327.9 0.9 fusion.8
  328.8 1.0 fusion.9
  329.8 1.4 pad_maximum_fusion.3
  331.2 2.2 pad_maximum_fusion.1
  333.3 0.5 broadcast.51
  333.9 0.7 reduce.9
  334.5 0.1 reshape.100
  334.7 1.0 fusion.60
  335.7 28.2 %all-to-all-done.1 = f32[32,2,2,3584]{3,2,1,0:T(2,128)} async-done(((f32[32,2,2,3584]{3,2,1,0:T(2,128)}), f32[32,2,2,3584]{3,2,1,0:T(2,128)}, u32[]{:S(2)}, u32[]{:S(2)}) %all-to-all-start.1) | async-done | bytes 1835040 | tf_op jit(solution)/shard_map/all_to_all | solution.py:109
  363.9 2.6 reshape.93
  366.4 1.6 convolution_convert_fusion.7
  (73 shorter events, 0.6 us)
Async XLA Ops:
  7.2 6.4 %copy-start.14 = (bf16[8,8]{1,0:T(8,128)(2,1)S(1)}, bf16[8,8]{1,0:T(8,128)(2,1)}, u32[]{:S(2)}) copy-start(bf16[8,8]{1,0:T(8,128)(2,1)} %param.9) | copy-start | bytes 388
  7.2 145.6 %all-gather.2.cloned.1.call-start = ((), (), s32[]{:S(2)}) async-start(), calls=%async_computation.5 | async-start | bytes 16809984 | tf_op jit(solution)/shard_map/all_gather | solution.py:84
  9.1 0.6 copy-start.8
  9.8 0.6 copy-start.6
  76.4 199.6 %reduce-scatter.4.cloned.1.call-start = ((), (), s32[]{:S(2)}) async-start(), calls=%async_computation.6 | async-start | bytes 8257536 | tf_op jit(solution)/shard_map/reduce_scatter | solution.py:98
  169.4 16.9 %copy-start = (bf16[2,3584,128]{2,1,0:T(8,128)(2,1)S(1)}, bf16[2,3584,128]{2,1,0:T(8,128)(2,1)}, u32[]{:S(2)}) copy-start(bf16[2,3584,128]{2,1,0:T(8,128)(2,1)} %param.11) | copy-start | bytes 5505028
  185.1 4.5 %copy-start.15 = (bf16[2,128,3584]{2,1,0:T(8,128)(2,1)S(1)}, bf16[2,128,3584]{2,1,0:T(8,128)(2,1)}, u32[]{:S(2)}) copy-start(bf16[2,128,3584]{2,1,0:T(8,128)(2,1)} %param.13) | copy-start | bytes 5505028
  186.3 6.7 %copy-start.10 = (f32[512]{0:T(512)}, f32[512]{0:T(512)S(1)}, u32[]{:S(2)}) copy-start(f32[512]{0:T(512)S(1)} %convert_reduce_fusion.1) | copy-start | bytes 6148
  186.3 6.7 %slice-start = ((s8[7471104]{0:T(1024)(128)(4,1)}), s8[4194304]{0:T(1024)(128)(4,1)S(1)}, s32[]{:S(2)}) async-start(s8[7471104]{0:T(1024)(128)(4,1)} %bitcast.80), calls=%async_computation.8 | async-start | bytes 8388608
  189.6 3.4 slice-start.1
  189.7 3.5 copy-start.1
  194.3 1.1 copy-start.3
  194.3 37.1 %copy-start.19 = (bf16[512,128]{1,0:T(8,128)(2,1)}, bf16[512,128]{1,0:T(8,128)(2,1)S(1)}, u32[]{:S(2)}) copy-start(bf16[512,128]{1,0:T(8,128)(2,1)S(1)} %get-tuple-element.7) | copy-start | bytes 393220
  199.6 103.3 %reduce-scatter.6.cloned.1.call-start = ((), (), s32[]{:S(2)}) async-start(), calls=%async_computation.7 | async-start | bytes 8257536 | tf_op jit(solution)/shard_map/reduce_scatter | solution.py:98
  215.5 4.6 %copy-start.16 = (bf16[2,128,3584]{2,1,0:T(8,128)(2,1)S(1)}, bf16[2,128,3584]{2,1,0:T(8,128)(2,1)}, u32[]{:S(2)}) copy-start(bf16[2,128,3584]{2,1,0:T(8,128)(2,1)} %param.13) | copy-start | bytes 5505028
  216.7 3.4 copy-start.12
  216.7 6.9 %slice-start.4 = ((s8[7471104]{0:T(1024)(128)(4,1)}), s8[4194304]{0:T(1024)(128)(4,1)S(1)}, s32[]{:S(2)}) async-start(s8[7471104]{0:T(1024)(128)(4,1)} %bitcast.84), calls=%async_computation.12 | async-start | bytes 8388608
  220.1 3.5 slice-start.5
  220.1 3.8 %copy-start.2 = (bf16[2,3584,128]{2,1,0:T(8,128)(2,1)S(1)}, bf16[2,3584,128]{2,1,0:T(8,128)(2,1)}, u32[]{:S(2)}) copy-start(bf16[2,3584,128]{2,1,0:T(8,128)(2,1)} %param.12) | copy-start | bytes 5505028
  225.0 1.1 copy-start.4
  225.0 10.2 %copy-start.21 = (bf16[512,128]{1,0:T(8,128)(2,1)}, bf16[512,128]{1,0:T(8,128)(2,1)S(1)}, u32[]{:S(2)}) copy-start(bf16[512,128]{1,0:T(8,128)(2,1)S(1)} %get-tuple-element.10) | copy-start | bytes 393220
  230.2 0.7 copy-start.18
  230.2 1.6 copy-start.17
  266.0 43.4 %all-to-all-start.2 = ((f32[32,1,4]{2,1,0:T(1,128)}), f32[32,1,4]{2,1,0:T(1,128)S(1)}, u32[]{:S(2)}, u32[]{:S(2)}) async-start(f32[32,1,4]{2,1,0:T(1,128)} %bitcast.11), calls=%async_computation.4 | async-start | bytes 32768 | tf_op jit(solution)/shard_map/all_to_all | solution.py:110
  305.6 17.5 %slice-start.2 = ((s8[7471104]{0:T(1024)(128)(4,1)}), s8[3276800]{0:T(1024)(128)(4,1)S(1)}, s32[]{:S(2)}) async-start(s8[7471104]{0:T(1024)(128)(4,1)} %bitcast.82), calls=%async_computation.10 | async-start | bytes 6553600
  309.3 54.5 %all-to-all-start.1 = ((f32[32,2,2,3584]{3,2,1,0:T(2,128)}), f32[32,2,2,3584]{3,2,1,0:T(2,128)}, u32[]{:S(2)}, u32[]{:S(2)}) async-start(f32[32,2,2,3584]{3,2,1,0:T(2,128)} %pad_maximum_fusion), calls=%async_computation.3 | async-start | bytes 3670016 | tf_op jit(solution)/shard_map/all_to_all | solution.py:109
  319.7 3.4 slice-start.3
  319.7 4.6 %slice-start.6 = ((s8[7471104]{0:T(1024)(128)(4,1)}), s8[4194304]{0:T(1024)(128)(4,1)S(1)}, s32[]{:S(2)}) async-start(s8[7471104]{0:T(1024)(128)(4,1)} %bitcast.86), calls=%async_computation.14 | async-start | bytes 8388608
  323.1 2.4 slice-start.7
  325.5 1.2 copy-start.5
  326.6 1.2 copy-start.11
  326.7 1.2 copy-start.20
  327.9 0.9 copy-start.13
  327.9 0.9 copy-start.22
  331.2 3.5 copy-start.9
  333.3 33.1 %copy-start.7 = (f32[8,128]{1,0:T(8,128)S(1)}, f32[8,128]{1,0:T(8,128)}, u32[]{:S(2)}) copy-start(f32[8,128]{1,0:T(8,128)} %copy-done.6) | copy-start | bytes 12292
Sparse Core Ops, SparseCore 0:
  76.6 76.1 all-gather.1
  199.7 50.7 reduce-scatter.3
  253.0 49.8 reduce-scatter.5
where the time goes:
time: 376 us; the launch traced here: 375 us
  waiting for transfers between devices  129 us (34%)
  blocking collectives  82.5 us (22%)
  local copies, waits for them, and re-layouts  71 us (19%)
  matrix products  45.7 us (12%)
  starting transfers between devices  20.7 us (6%)
  between operations  14.3 us (4%)
  other arithmetic  11.5 us (3%)
    all_gather x1, waiting for transfers between devices, local(): recv = lax.all_gather(recv, 'dp', axis=0, tiled=True)  76.3 us
    all_to_all x1, blocking collectives, local(): lax.all_to_all(send, 'expert', split_axis=0, concat_axis=0, tiled=True)  57.3 us
    reshape x2, local copies, waits for them, and re-layouts, local(): recv[:, j * capacity:(j + 1) * capacity, :].reshape(rows * capacity, -1)  31.4 us
    all_to_all x1, waiting for transfers between devices, local(): lax.all_to_all(token_part, 'expert', split_axis=0, concat_axis=0, tiled=T...  28.2 us
    unnamed x1, blocking collectives  25.2 us
    reduce_scatter x2, waiting for transfers between devices, local(): part = lax.psum_scatter(token_part, 'dp', scatter_dimension=0, tiled=False)  24.2 us
    slice x1, local copies, waits for them, and re-layouts, local(): recv[:, j * capacity:(j + 1) * capacity, :].reshape(rows * capacity, -1)  16.6 us
    all_to_all x1, starting transfers between devices, local(): lax.all_to_all(token_part, 'expert', split_axis=0, concat_axis=0, tiled=T...  10.3 us
  transfers between devices with their start and end apart: 5, of which 3 were waited for; matrix products, arithmetic and copies ran while one was open for 17% of the time, Pallas kernels for 0%

commit v1 on v0

--- a/solution.py
+++ b/solution.py
@@ -1,3 +1,4 @@
+import functools
 from functools import partial
 import jax
 import jax.numpy as jnp
@@ -5,6 +6,18 @@
 from jax.sharding import PartitionSpec as P
 
 TOPK = 8
+
+
+def balance_desk(local_values, along_axis):
+    return jnp.concatenate(
+        lax.all_to_all(
+            jnp.stack([local_values for _ in range(lax.axis_size(along_axis))]), along_axis, 0, 0
+        ),
+        0,
+    )
+
+
+keep_up_block = functools.partial(balance_desk, along_axis="dp")
 
 
 def route_table(routes, experts_all, capacity):
@@ -81,7 +94,7 @@
     send = dispatch(table, tokens, cotangent, gates)
     send = send.reshape(n_expert, per_dest, send.shape[-1])
     recv = lax.all_to_all(send, "expert", split_axis=0, concat_axis=0, tiled=True)
-    recv = lax.all_gather(recv, "dp", axis=0, tiled=True)
+    recv = keep_up_block(recv)
     rows = n_groups * n_expert
     parts, gparts, grads_g, grads_u, grads_d = ([], [], [], [], [])
     for j in range(local_experts):

time: 376 us -> 469 us (1.25)
  blocking collectives: 82.5 us -> 251 us
  waiting for transfers between devices: 129 us -> 53.7 us
  starting transfers between devices: 20.7 us -> 15.7 us
    all_to_all x0 -> x1, blocking collectives: none -> 169 us  [balance_desk(): lax.all_to_all(jnp.stack([local_values for _ in range(lax.axis_size(along...]
    all_gather x1 -> x0, waiting for transfers between devices: 76.3 us -> none  [local(): recv = lax.all_gather(recv, 'dp', axis=0, tiled=True)]
    all_to_all x1, starting transfers between devices: 10.1 us -> 5.17 us  [local(): lax.all_to_all(gate_part, 'expert', split_axis=0, concat_axis=0, tiled=True)]
  transfers between devices with their start and end apart: 5 -> 4, of which waited for: 3 -> 2; matrix products, arithmetic and copies ran while one was open for 17% -> 13% of each run, Pallas kernels for 0% -> 0%
where the time goes in v1:
time: 469 us; the launch traced here: 468 us
  blocking collectives  251 us (54%)
  local copies, waits for them, and re-layouts  75.5 us (16%)
  waiting for transfers between devices  53.7 us (11%)
  matrix products  45.7 us (10%)
  starting transfers between devices  15.7 us (3%)
  between operations  14.6 us (3%)
  other arithmetic  11.5 us (2%)
    all_to_all x1, blocking collectives, balance_desk(): lax.all_to_all(jnp.stack([local_values for _ in range(lax.axis_size(along...  169 us
    all_to_all x1, blocking collectives, local(): lax.all_to_all(send, 'expert', split_axis=0, concat_axis=0, tiled=True)  57.2 us
    reshape x2, local copies, waits for them, and re-layouts, local(): recv[:, j * capacity:(j + 1) * capacity, :].reshape(rows * capacity, -1)  31.4 us
    all_to_all x1, waiting for transfers between devices, local(): lax.all_to_all(token_part, 'expert', split_axis=0, concat_axis=0, tiled=T...  28.2 us
    reduce_scatter x2, waiting for transfers between devices, local(): part = lax.psum_scatter(token_part, 'dp', scatter_dimension=0, tiled=False)  25.5 us
    unnamed x1, blocking collectives  24.4 us
    slice x1, local copies, waits for them, and re-layouts, local(): recv[:, j * capacity:(j + 1) * capacity, :].reshape(rows * capacity, -1)  16.5 us
    all_to_all x1, starting transfers between devices, local(): lax.all_to_all(token_part, 'expert', split_axis=0, concat_axis=0, tiled=T...  10.3 us
  transfers between devices with their start and end apart: 4, of which 2 were waited for; matrix products, arithmetic and copies ran while one was open for 13% of the time, Pallas kernels for 0%

profile of v1, /device:TPU:32, one launch (start us, length us, event | category | flops | bytes accessed | tf_op | source)
XLA Modules:
  0.0 467.5 jit_solution(10736302597373295422)
XLA Ops:
  7.2 0.8 eq.57
  8.2 0.2 select_reduce_fusion
  8.4 0.7 multiply_add_fusion
  9.1 0.6 copy-done.8
  9.8 0.6 copy-done.6
  10.4 1.5 convolution_convert_fusion
  11.9 1.6 concatenate.12
  13.6 0.2 fusion.22
  13.8 0.2 concatenate.15
  14.1 5.0 %concatenate.14 = bf16[32,4,7296]{2,1,0:T(4,128)(2,1)S(1)} concatenate(bf16[32,4,7168]{2,1,0:T(4,128)(2,1)} %concatenate.12, bf16[32,4,1]{2,1,0:T(4,128)(2,1)S(1)} %concatenate.15, bf16[32,4,127]{2,1,0:T(4,128)(2,1)S(1)} %broadcast_in_dim.2), dimensions={2} | concatenate | bytes 3735552 | tf_op jit(solution)/shard_map/concatenate | solution.py:46
  19.1 57.2 %all_to_all.24 = bf16[32,4,7296]{2,1,0:T(4,128)(2,1)S(1)} all-to-all(bf16[32,4,7296]{2,1,0:T(4,128)(2,1)S(1)} %concatenate.14), channel_id=1, replica_groups=mesh['dp'=8,'expert'=32] {'expert'}, dimensions={0} | all-to-all | bytes 3735552 | tf_op jit(solution)/shard_map/all_to_all | solution.py:96
  76.3 4.6 stack.44
  80.9 169.2 %all_to_all.25 = bf16[8,32,4,7296]{3,2,1,0:T(4,128)(2,1)} all-to-all(bf16[8,32,4,7296]{3,2,1,0:T(4,128)(2,1)S(1)} %stack.44), channel_id=1, replica_groups=mesh['dp'=8,'expert'=32] {'dp'}, dimensions={0} | all-to-all | bytes 29884416 | tf_op jit(solution)/shard_map/all_to_all | solution.py:13
  250.1 16.5 %fusion.66 = (bf16[256,2,7296]{2,1,0:T(2,128)(2,1)}, bf16[256,2,7296]{2,1,0:T(2,128)(2,1)}) fusion(bf16[256,4,7296]{2,1,0:T(4,128)(2,1)} %bitcast.79), kind=kLoop, calls=%fused_computation.100 | loop fusion | bytes 29884416 | tf_op jit(solution)/shard_map/slice | solution.py:101
  266.6 15.7 %reshape.95 = bf16[512,7296]{1,0:T(8,128)(2,1)} reshape(bf16[256,2,7296]{2,1,0:T(2,128)(2,1)} %get-tuple-element.5) | data formatting | bytes 14942208 | tf_op jit(solution)/shard_map/reshape | solution.py:101
  282.4 1.2 convert_reduce_fusion.1
  283.5 3.3 fusion.18
  286.9 3.4 fusion.27
  290.3 0.1 copy-done.1
  290.4 1.1 multiply_convert_fusion.1
  291.6 1.1 fusion.36
  292.7 4.1 convolution_add_fusion.1
  296.8 0.2 reduce-scatter.6.cloned.1.call-start
  297.0 15.7 %reshape.97 = bf16[512,7296]{1,0:T(8,128)(2,1)} reshape(bf16[256,2,7296]{2,1,0:T(2,128)(2,1)} %get-tuple-element.6) | data formatting | bytes 14942208 | tf_op jit(solution)/shard_map/reshape | solution.py:101
  312.7 1.2 convert_reduce_fusion
  313.9 3.4 fusion.12
  317.3 3.4 fusion.24
  320.8 0.3 copy-done.2
  321.0 1.1 multiply_convert_fusion
  322.2 1.1 fusion.29
  323.3 4.1 convolution_add_fusion
  327.4 0.6 copy-done.18
  328.1 0.6 dynamic-slice
  328.7 0.3 copy-done.17
  328.9 3.3 fusion.1
  332.2 0.1 stack_reshape.6
  332.4 3.3 fusion.3
  335.7 0.1 stack_reshape.7
  335.9 0.5 copy.21
  336.4 24.4 %all-reduce = f32[8,128]{0,1:T(8,128)S(1)} all-reduce(f32[8,128]{0,1:T(8,128)S(1)} %bitcast.90), channel_id=4, replica_groups=mesh['dp'=8,'expert'=32] {'dp'}, use_global_device_ids=true, to_apply=%region_7.8.clone | all-reduce | flops 1024 | bytes 8192
  360.8 0.8 dynamic-slice_reduce_fusion
  361.6 0.7 all_to_all.18
  362.3 5.2 %all-to-all-start.3 = ((f32[32,1,4]{2,1,0:T(1,128)}), f32[32,1,4]{2,1,0:T(1,128)S(1)}, u32[]{:S(2)}, u32[]{:S(2)}) async-start(f32[32,1,4]{2,1,0:T(1,128)} %bitcast.12), calls=%async_computation.5 | async-start | bytes 32768 | tf_op jit(solution)/shard_map/all_to_all | solution.py:123
  367.5 2.6 stack_reshape_reduce_scatter.6
  370.2 25.4 %reduce-scatter.6.cloned.1.call-done = f32[1,64,3584]{2,1,0:T(8,128)} async-done(((f32[8,64,3584]{2,1,0:T(8,128)}), f32[1,64,3584]{2,1,0:T(8,128)}) %reduce-scatter.6.cloned.1.call-update) | async-done | bytes 917520 | tf_op jit(solution)/shard_map/reduce_scatter | solution.py:111
  395.6 2.6 stack_reshape_reduce_scatter.7
  398.3 3.8 pad_maximum_fusion
  402.1 10.3 %all-to-all-start.2 = ((f32[32,2,2,3584]{3,2,1,0:T(2,128)}), f32[32,2,2,3584]{3,2,1,0:T(2,128)}, u32[]{:S(2)}, u32[]{:S(2)}) async-start(f32[32,2,2,3584]{3,2,1,0:T(2,128)} %pad_maximum_fusion), calls=%async_computation.4 | async-start | bytes 3670016 | tf_op jit(solution)/shard_map/all_to_all | solution.py:122
  412.4 3.4 fusion.6
  415.8 1.2 fusion.4
  417.0 1.2 slice-done.7
  418.1 1.2 fusion.5
  419.3 1.2 fusion.7
  420.5 0.9 fusion.8
  421.5 1.0 fusion.9
  422.5 1.4 pad_maximum_fusion.3
  423.9 2.2 pad_maximum_fusion.1
  426.0 0.5 broadcast.53
  426.5 0.7 reduce.9
  427.2 0.1 reshape.106
  427.3 1.0 fusion.60
  428.3 28.2 %all-to-all-done.2 = f32[32,2,2,3584]{3,2,1,0:T(2,128)} async-done(((f32[32,2,2,3584]{3,2,1,0:T(2,128)}), f32[32,2,2,3584]{3,2,1,0:T(2,128)}, u32[]{:S(2)}, u32[]{:S(2)}) %all-to-all-start.2) | async-done | bytes 1835040 | tf_op jit(solution)/shard_map/all_to_all | solution.py:122
  456.5 2.6 reshape.99
  459.1 1.6 convolution_convert_fusion.7
  (72 shorter events, 0.7 us)
Async XLA Ops:
  7.2 6.4 %copy-start.14 = (bf16[8,8]{1,0:T(8,128)(2,1)S(1)}, bf16[8,8]{1,0:T(8,128)(2,1)}, u32[]{:S(2)}) copy-start(bf16[8,8]{1,0:T(8,128)(2,1)} %param.9) | copy-start | bytes 388
  7.2 360.4 %reduce-scatter.4.cloned.1.call-start = ((), (), s32[]{:S(2)}) async-start(), calls=%async_computation.6 | async-start | bytes 8257536 | tf_op jit(solution)/shard_map/reduce_scatter | solution.py:111
  9.1 0.6 copy-start.8
  9.8 0.6 copy-start.6
  266.6 16.9 %copy-start = (bf16[2,3584,128]{2,1,0:T(8,128)(2,1)S(1)}, bf16[2,3584,128]{2,1,0:T(8,128)(2,1)}, u32[]{:S(2)}) copy-start(bf16[2,3584,128]{2,1,0:T(8,128)(2,1)} %param.11) | copy-start | bytes 5505028
  282.4 4.5 copy-start.15
  283.5 6.7 %copy-start.10 = (f32[512]{0:T(512)}, f32[512]{0:T(512)S(1)}, u32[]{:S(2)}) copy-start(f32[512]{0:T(512)S(1)} %convert_reduce_fusion.1) | copy-start | bytes 6148
  283.5 6.7 %slice-start = ((s8[7471104]{0:T(1024)(128)(4,1)}), s8[4194304]{0:T(1024)(128)(4,1)S(1)}, s32[]{:S(2)}) async-start(s8[7471104]{0:T(1024)(128)(4,1)} %bitcast.82), calls=%async_computation.8 | async-start | bytes 8388608
  286.9 3.4 slice-start.1
  286.9 3.5 copy-start.1
  291.5 1.1 copy-start.3
  291.5 37.1 %copy-start.19 = (bf16[512,128]{1,0:T(8,128)(2,1)}, bf16[512,128]{1,0:T(8,128)(2,1)S(1)}, u32[]{:S(2)}) copy-start(bf16[512,128]{1,0:T(8,128)(2,1)S(1)} %get-tuple-element.7) | copy-start | bytes 393220
  296.8 98.8 %reduce-scatter.6.cloned.1.call-start = ((), (), s32[]{:S(2)}) async-start(), calls=%async_computation.7 | async-start | bytes 8257536 | tf_op jit(solution)/shard_map/reduce_scatter | solution.py:111
  312.7 4.6 copy-start.16
  313.9 3.4 copy-start.12
  313.9 6.9 %slice-start.4 = ((s8[7471104]{0:T(1024)(128)(4,1)}), s8[4194304]{0:T(1024)(128)(4,1)S(1)}, s32[]{:S(2)}) async-start(s8[7471104]{0:T(1024)(128)(4,1)} %bitcast.86), calls=%async_computation.12 | async-start | bytes 8388608
  317.3 3.5 slice-start.5
  317.3 3.7 copy-start.2
  322.2 1.1 copy-start.4
  322.2 10.2 %copy-start.21 = (bf16[512,128]{1,0:T(8,128)(2,1)}, bf16[512,128]{1,0:T(8,128)(2,1)S(1)}, u32[]{:S(2)}) copy-start(bf16[512,128]{1,0:T(8,128)(2,1)S(1)} %get-tuple-element.10) | copy-start | bytes 393220
  327.4 0.7 copy-start.18
  327.4 1.5 copy-start.17
  362.3 39.7 %all-to-all-start.3 = ((f32[32,1,4]{2,1,0:T(1,128)}), f32[32,1,4]{2,1,0:T(1,128)S(1)}, u32[]{:S(2)}, u32[]{:S(2)}) async-start(f32[32,1,4]{2,1,0:T(1,128)} %bitcast.12), calls=%async_computation.5 | async-start | bytes 32768 | tf_op jit(solution)/shard_map/all_to_all | solution.py:123
  398.3 17.5 %slice-start.2 = ((s8[7471104]{0:T(1024)(128)(4,1)}), s8[3276800]{0:T(1024)(128)(4,1)S(1)}, s32[]{:S(2)}) async-start(s8[7471104]{0:T(1024)(128)(4,1)} %bitcast.84), calls=%async_computation.10 | async-start | bytes 6553600
  402.1 54.5 %all-to-all-start.2 = ((f32[32,2,2,3584]{3,2,1,0:T(2,128)}), f32[32,2,2,3584]{3,2,1,0:T(2,128)}, u32[]{:S(2)}, u32[]{:S(2)}) async-start(f32[32,2,2,3584]{3,2,1,0:T(2,128)} %pad_maximum_fusion), calls=%async_computation.4 | async-start | bytes 3670016 | tf_op jit(solution)/shard_map/all_to_all | solution.py:122
  412.3 3.4 slice-start.3
  412.4 4.6 slice-start.6
  415.8 2.4 slice-start.7
  418.1 1.2 copy-start.5
  419.3 1.2 copy-start.11
  419.3 1.2 copy-start.20
  420.5 0.9 copy-start.13
  420.5 0.9 copy-start.22
  423.8 3.5 copy-start.9
  426.0 33.1 %copy-start.7 = (f32[8,128]{1,0:T(8,128)S(1)}, f32[8,128]{1,0:T(8,128)}, u32[]{:S(2)}) copy-start(f32[8,128]{1,0:T(8,128)} %copy-done.6) | copy-start | bytes 12292
Sparse Core Ops, SparseCore 0:
  296.9 46.0 reduce-scatter.3
  345.6 49.9 reduce-scatter.5
